TPU v7x, 32 devices: a whole 2x2x4 slice. The times are simulated.
32 devices in a mesh: lat: 4 (over x, core), lon: 8 (over z, y).
Axes of the slice: x: 2, y: 2, z: 4, core: 2. Of those that a mesh axis runs over, the one named last changes fastest.
Arguments:
- field: bfloat16 [64, 256, 1024], P('lat', 'lon'), may hold values from -600 to 600
- norm_gain: float32 [1024], replicated, may hold values from 0.1 to 1.9
- w_qkv: bfloat16 [1024, 3072], replicated, may hold values from -2 to 2
- w_out: bfloat16 [1024, 1024], replicated, may hold values from -0.1875 to 0.1875
- block_cols: int32 [4, 4], replicated, may hold values from 1 to 7, as said below
- antipode: int32 [256], P('lon'), may hold values from 0 to 255, as said below
Outputs:
- update: bfloat16 [64, 256, 1024], P('lat', 'lon')
Inputs may be any that keep to these rules, and one draw needn't show every extreme that they name: `block_cols`: each row lists 4 different blocks b with |b - 4 - row| <= 3. A permutation of the longitudes; antipode[l] // 32 equals (l // 32 + 256 // 64) modulo 256 // 32.
All inputs are finite; a program needn't handle non-finite values.
Results may differ from a plain program's by a relative error of at most 0.005.
The roundings to bfloat16 on the way count: a program that leaves them out, or rounds other values in their place, can miss the bound.
Values may be sent and summed in bfloat16 or wider, within the bound.
A program may use at most 128 MiB of HBM per device.

v0:
```python
import jax
import jax.numpy as jnp
from jax import lax
from jax.sharding import PartitionSpec as P

HEADS = 16
HD = 64
HZ = 8
BM = 8
epsilon = 1e-06


def shifted(shard, axis, by):
    devices = lax.axis_size(axis)
    return lax.ppermute(shard, axis, [(i, (i + by) % devices) for i in range(devices)])


def from_partner(value, axis, distance):
    mask = 2**distance
    pairs = [(source, source ^ mask) for source in range(lax.axis_size(axis))]
    return lax.ppermute(value, axis, pairs)


def softmax_rows(scores):
    row_max = jnp.max(scores, axis=-1, keepdims=True)
    exponent = jnp.exp(scores - row_max)
    return (exponent / jnp.sum(exponent, axis=-1, keepdims=True)).astype(jnp.bfloat16)


def zonal_attend(query_rows, key_rows, value_rows):
    item_count, length, pair_width = query_rows.shape
    score_scale = HD ** (-0.5)
    query_heads = query_rows.reshape(item_count, length, 2, HD)
    key_heads = key_rows.reshape(item_count, length, 2, HD)
    value_heads = value_rows.reshape(item_count, length, 2, HD)
    block_rows = min(512, length)
    pieces = []
    for first_row in range(0, length, block_rows):
        query_block = query_heads[:, first_row : first_row + block_rows]
        scores = (
            jnp.einsum(
                "iqhd,ikhd->ihqk", query_block, key_heads, preferred_element_type=jnp.float32
            )
            * score_scale
        )
        soft_weights = softmax_rows(scores)
        result = jnp.einsum(
            "ihqk,ikhd->iqhd", soft_weights, value_heads, preferred_element_type=jnp.float32
        )
        pieces.append(result.astype(jnp.bfloat16))
    return jnp.concatenate(pieces, axis=1).reshape(item_count, length, pair_width)


def on_device(field, norm_gain, w_qkv, w_out, block_cols, antipode):
    cycle_count, lon_count, channels = field.shape
    column_heads = HEADS - HZ
    pair_count = HZ // 2
    zonal_width = HZ * HD
    score_scale = HD ** (-0.5)
    values = field.astype(jnp.float32)
    scaled = values * lax.rsqrt(jnp.mean(values * values, axis=-1, keepdims=True) + epsilon)
    normed = (scaled * norm_gain).astype(jnp.bfloat16)
    weight_split = w_qkv.reshape(channels, 3, channels)
    zonal_weight = weight_split[:, :, :zonal_width].reshape(channels, 3, pair_count, 2 * HD)
    column_weight = weight_split[:, :, zonal_width:]
    zonal_part = jnp.einsum(
        "rld,dtpc->trplc", normed, zonal_weight, preferred_element_type=jnp.float32
    )
    zonal_part = zonal_part.astype(jnp.bfloat16).reshape(
        3, cycle_count * pair_count, lon_count, 2 * HD
    )
    column_proj = jnp.einsum(
        "rld,dtc->rltc", normed, column_weight, preferred_element_type=jnp.float32
    ).astype(jnp.bfloat16)
    query_all, key_all, value_all = (
        lax.all_to_all(zonal_part[0], "lon", split_axis=0, concat_axis=1, tiled=True),
        lax.all_to_all(zonal_part[1], "lon", split_axis=0, concat_axis=1, tiled=True),
        lax.all_to_all(zonal_part[2], "lon", split_axis=0, concat_axis=1, tiled=True),
    )
    zonal_items = zonal_attend(query_all, key_all, value_all)
    returned = lax.all_to_all(zonal_items, "lon", split_axis=1, concat_axis=0, tiled=True)
    zonal_out = returned.reshape(cycle_count, pair_count, lon_count, 2 * HD)
    cap_half = lax.axis_index("lat") % 2
    lon_devices = lax.axis_size("lon")
    merged = column_proj[:, :, 1:]

    def cap_order(own_rows, other_rows):
        return jnp.where(
            cap_half == 0,
            jnp.concatenate([own_rows, other_rows], axis=0),
            jnp.concatenate([other_rows, own_rows], axis=0),
        )

    far_own = shifted(merged, "lon", lon_devices // 2)
    partner, far_partner = from_partner((merged, far_own), "lat", 0)
    cap_rows = cap_order(merged, partner)
    far_side = cap_order(far_own, far_partner)
    across = jnp.take(far_side, antipode % lon_count, axis=1)[::-1]
    column = jnp.concatenate([across, cap_rows], axis=0)
    block_total = column.shape[0] // BM
    column = column.reshape(block_total, BM, lon_count, 2, column_heads, HD)
    picks_per_row = block_cols.shape[1]
    local_blocks = cycle_count // BM
    pieces = []
    for local_block in range(local_blocks):
        block_row = cap_half * local_blocks + local_block
        picked = lax.dynamic_index_in_dim(block_cols, block_row, 0, keepdims=False)
        chosen = jnp.take(column, picked, axis=0).reshape(
            picks_per_row * BM, lon_count, 2, column_heads, HD
        )
        query_block = column_proj[local_block * BM : (local_block + 1) * BM, :, 0]
        query_block = query_block.reshape(BM, lon_count, column_heads, HD)
        scores = (
            jnp.einsum(
                "qlhd,klhd->lhqk", query_block, chosen[:, :, 0], preferred_element_type=jnp.float32
            )
            * score_scale
        )
        soft_weights = softmax_rows(scores)
        result = jnp.einsum(
            "lhqk,klhd->qlhd", soft_weights, chosen[:, :, 1], preferred_element_type=jnp.float32
        )
        pieces.append(result.astype(jnp.bfloat16).reshape(BM, lon_count, column_heads * HD))
    meridional = jnp.concatenate(pieces, axis=0)
    zonal_rows_out = w_out[:zonal_width].reshape(pair_count, 2 * HD, channels)
    total = jnp.einsum(
        "rplc,pce->rle", zonal_out, zonal_rows_out, preferred_element_type=jnp.float32
    )
    total = total + jnp.einsum(
        "rlc,ce->rle", meridional, w_out[zonal_width:], preferred_element_type=jnp.float32
    )
    return total.astype(jnp.bfloat16)


def solution(mesh):
    in_specs = (P("lat", "lon", None), P(), P(), P(), P(), P("lon"))
    out_specs = P("lat", "lon", None)
    return jax.shard_map(
        on_device, mesh=mesh, in_specs=in_specs, out_specs=out_specs, check_vma=False
    )
```

profile of v0, /device:TPU:1, one launch (start us, length us, event | category | flops | bytes accessed | tf_op | source)
XLA Modules:
  0.0 214.1 jit_solution(12262498181520285386)
XLA Ops:
  1.5 8.6 %copy.53 = bf16[1024,3072]{0,1:T(8,128)(2,1)} copy(bf16[1024,3072]{1,0:T(8,128)(2,1)} %param.10) | data formatting | bytes 12582912 | tf_op args[2]
  10.1 2.3 %slice.65 = bf16[1024,3,512]{0,2,1:T(8,128)(2,1)S(1)} slice(bf16[1024,3,1024]{0,2,1:T(8,128)(2,1)} %bitcast.123), slice={[0:1024], [0:3], [0:512]} | slice | bytes 6291456 | tf_op jit(solution)/shard_map/slice | solution.py:64
  12.4 1.9 fusion.19
  15.5 19.8 %all_to_all.60 = bf16[64,32,128]{2,1,0:T(8,128)(2,1)S(1)} all-to-all(bf16[64,32,128]{2,1,0:T(8,128)(2,1)S(1)} %bitcast.137), channel_id=1, replica_groups=mesh['lat'=4,'lon'=8] {'lon'}, dimensions={0} | all-to-all | bytes 1048576 | tf_op jit(solution)/shard_map/all_to_all | solution.py:77
  35.3 17.5 %all_to_all.61 = bf16[64,32,128]{2,1,0:T(8,128)(2,1)S(1)} all-to-all(bf16[64,32,128]{2,1,0:T(8,128)(2,1)S(1)} %bitcast.136), channel_id=1, replica_groups=mesh['lat'=4,'lon'=8] {'lon'}, dimensions={0} | all-to-all | bytes 1048576 | tf_op jit(solution)/shard_map/all_to_all | solution.py:78
  52.8 4.1 %all-to-all-start.1 = ((bf16[64,32,128]{2,1,0:T(8,128)(2,1)}), bf16[64,32,128]{2,1,0:T(8,128)(2,1)S(1)}, u32[]{:S(2)}, u32[]{:S(2)}) async-start(bf16[64,32,128]{2,1,0:T(8,128)(2,1)} %bitcast.9), calls=%async_computation.1 | async-start | bytes 1048576 | tf_op jit(solution)/shard_map/all_to_all | solution.py:76
  56.9 3.8 %fusion.18 = bf16[16,32,3,512]{3,1,2,0:T(8,128)(2,1)S(1)} fusion(bf16[1024,3,1024]{0,2,1:T(8,128)(2,1)} %bitcast.124, bf16[16,32,1024]{2,1,0:T(8,128)(2,1)S(1)} %copy-done.5, f32[1024]{0:T(1024)S(1)} %copy-done.7, f32[16,32]{1,0:T(8,128)S(1)} %add_rsqrt_fusion), kind=kOutput, calls=%fused_computation.38 | convolution fusion | flops 1613496320 | bytes 5773312 | tf_op jit(solution)/shard_map/rld,dtc->rltc/dot_general | solution.py:72
  62.3 2.6 %collective-permute-start = (bf16[16,32,2,512]{3,1,2,0:T(8,128)(2,1)S(1)}, bf16[16,32,2,512]{3,1,2,0:T(8,128)(2,1)}, u32[]{:S(2)}, u32[]{:S(2)}) collective-permute-start(bf16[16,32,2,512]{3,1,2,0:T(8,128)(2,1)S(1)} %slice.70), channel_id=1, source_target_pairs={{0,4},{1,5},{2,6},{3,7},{4,0},{5,1},{6,2},{7,3},{8,12},{9,13},{10,... | collective-permute-start | bytes 3145736 | tf_op jit(solution)/shard_map/ppermute | solution.py:15
  65.8 26.7 %all-to-all-done.1 = bf16[64,32,128]{2,1,0:T(8,128)(2,1)S(1)} async-done(((bf16[64,32,128]{2,1,0:T(8,128)(2,1)}), bf16[64,32,128]{2,1,0:T(8,128)(2,1)S(1)}, u32[]{:S(2)}, u32[]{:S(2)}) %all-to-all-start.1) | async-done | bytes 524320 | tf_op jit(solution)/shard_map/all_to_all | solution.py:76
  94.3 2.4 %reshape.79 = bf16[8,256,2,64]{3,2,1,0:T(2,128)(2,1)S(1)} reshape(bf16[8,8,32,128]{3,2,1,0:T(8,128)(2,1)} %copy.57) | data formatting | bytes 1048576 | tf_op jit(solution)/shard_map/reshape | solution.py:34
  97.5 3.2 %fusion.56 = (f32[8,2,256]{2,1,0:T(2,128)S(1)}, f32[8,2,256,256]{2,3,1,0:T(8,128)S(1)}) fusion(f32[8,2,256,256]{2,3,1,0:T(8,128)S(1)} %fusion.36), kind=kOutput, calls=%fused_computation.90 | output fusion | flops 4194559 | bytes 8404992 | tf_op jit(solution)/shard_map/sub | solution.py:26
  102.4 5.0 %all-to-all-start.3 = ((bf16[8,256,128]{2,0,1:T(8,128)(2,1)}), bf16[8,256,128]{2,0,1:T(8,128)(2,1)S(1)}, u32[]{:S(2)}, u32[]{:S(2)}) async-start(bf16[8,256,128]{2,0,1:T(8,128)(2,1)} %copy.62), calls=%async_computation.3 | async-start | bytes 1048576 | tf_op jit(solution)/shard_map/all_to_all | solution.py:81
  107.3 13.7 %collective-permute-done = bf16[16,32,2,512]{3,1,2,0:T(8,128)(2,1)} collective-permute-done((bf16[16,32,2,512]{3,1,2,0:T(8,128)(2,1)S(1)}, bf16[16,32,2,512]{3,1,2,0:T(8,128)(2,1)}, u32[]{:S(2)}, u32[]{:S(2)}) %collective-permute-start) | collective-permute-done | bytes 1048608 | tf_op jit(solution)/shard_map/ppermute | solution.py:15
  121.0 3.8 %collective-permute-start.1 = (bf16[16,32,2,512]{3,1,2,0:T(8,128)(2,1)}, bf16[16,32,2,512]{3,1,2,0:T(8,128)(2,1)}, u32[]{:S(2)}, u32[]{:S(2)}) collective-permute-start(bf16[16,32,2,512]{3,1,2,0:T(8,128)(2,1)} %collective-permute-done), channel_id=1, source_target_pairs={{0,8},{8,0},{16,24},{24,16},{1,9},{9,1},{17,25},{25,17},{2,10},{10... | collective-permute-start | bytes 3145736 | tf_op jit(solution)/shard_map/ppermute | solution.py:21
  126.7 3.2 %maximum_select_fusion.1 = bf16[32,32,2,512]{3,1,2,0:T(8,128)(2,1)} fusion(bf16[16,32,2,512]{3,1,2,0:T(8,128)(2,1)} %collective-permute-done.2, bf16[16,32,2,512]{3,1,2,0:T(8,128)(2,1)S(1)} %slice.70, pred[]{:T(512)S(6)} %eq.8), kind=kLoop, calls=%fused_computation.31 | loop fusion | flops 3145728 | bytes 4194305 | tf_op jit(solution)/shard_map/jit(_where)/select_n | solution.py:88
  130.8 2.6 %maximum_select_fusion = bf16[32,32,2,512]{3,1,2,0:T(8,128)(2,1)S(1)} fusion(bf16[16,32,2,512]{3,1,2,0:T(8,128)(2,1)} %collective-permute-done.1, bf16[16,32,2,512]{3,1,2,0:T(8,128)(2,1)} %collective-permute-done, pred[]{:T(512)S(6)} %eq.8), kind=kLoop, calls=%fused_computation.30 | loop fusion | flops 3145728 | bytes 4194305 | tf_op jit(solution)/shard_map/jit(_where)/select_n | solution.py:88
  133.4 2.5 %copy.66 = bf16[32,32,2,512]{3,0,2,1:T(8,128)(2,1)} copy(bf16[32,32,2,512]{3,1,2,0:T(8,128)(2,1)S(1)} %maximum_select_fusion) | data formatting | bytes 4194304 | tf_op jit(solution)/shard_map/jit(_where)/select_n | solution.py:88
  135.8 2.3 %gather_fusion = bf16[32,32,2,512]{3,1,2,0:T(8,128)(2,1)S(1)} fusion(bf16[32,32,2,512]{3,0,2,1:T(8,128)(2,1)} %copy.66, s32[1024]{0:T(1024)S(1)} %pad_clamp_fusion.2), kind=kCustom, calls=%fused_computation.2 | custom fusion | bytes 4194432 | tf_op jit(solution)/shard_map/jit(_take)/gather | solution.py:98
  138.1 3.8 %fusion.15 = bf16[32,32,2,512]{3,1,2,0:T(8,128)(2,1)} fusion(bf16[32,32,2,512]{3,1,2,0:T(8,128)(2,1)S(1)} %gather_fusion, pred[32]{0:T(512)(128)(4,1)S(1)} %get-tuple-element.10), kind=kLoop, calls=%fused_computation.35 | loop fusion | flops 1048576 | bytes 4194336 | tf_op jit(solution)/shard_map/jit(_take)/select_n | solution.py:98
  141.9 3.3 %rev.3 = bf16[32,32,2,512]{3,1,2,0:T(8,128)(2,1)} reverse(bf16[32,32,2,512]{3,1,2,0:T(8,128)(2,1)} %fusion.15), dimensions={0} | reverse | bytes 4194304 | tf_op jit(solution)/shard_map/rev | solution.py:98
  145.2 3.9 %pad_maximum_fusion = bf16[64,32,2,512]{3,1,2,0:T(8,128)(2,1)} fusion(bf16[32,32,2,512]{3,1,2,0:T(8,128)(2,1)S(1)} %copy-done, bf16[32,32,2,512]{3,1,2,0:T(8,128)(2,1)} %rev.3), kind=kLoop, calls=%fused_computation.6 | loop fusion | flops 2097152 | bytes 8388608 | tf_op jit(solution)/shard_map/concatenate | solution.py:99
  149.1 11.2 %reshape.83 = bf16[8,8,32,2,8,64]{5,4,2,3,1,0:T(8,128)(2,1)} reshape(bf16[64,32,2,512]{3,1,2,0:T(8,128)(2,1)} %pad_maximum_fusion) | data formatting | bytes 8388608 | tf_op jit(solution)/shard_map/reshape | solution.py:101
  160.3 6.4 %gather_fusion.2 = bf16[4,8,32,2,8,64]{5,4,2,3,1,0:T(8,128)(2,1)} fusion(bf16[8,8,32,2,8,64]{5,4,2,3,1,0:T(8,128)(2,1)} %reshape.83, s32[1024]{0:T(1024)S(1)} %pad_clamp_fusion), kind=kCustom, calls=%fused_computation.1.clone | custom fusion | bytes 4194320 | tf_op jit(solution)/shard_map/jit(_take)/gather | solution.py:108
  166.7 6.4 %gather_fusion.1 = bf16[4,8,32,2,8,64]{5,4,2,3,1,0:T(8,128)(2,1)} fusion(bf16[8,8,32,2,8,64]{5,4,2,3,1,0:T(8,128)(2,1)} %reshape.83, s32[1024]{0:T(1024)S(1)} %pad_clamp_fusion.1), kind=kCustom, calls=%fused_computation.clone | custom fusion | bytes 4194320 | tf_op jit(solution)/shard_map/jit(_take)/gather | solution.py:108
  173.1 6.2 %broadcast_select_fusion = (bf16[4,8,32,2,8,64]{5,4,2,3,1,0:T(8,128)(2,1)S(1)}, bf16[4,8,32,2,8,64]{5,4,2,3,1,0:T(8,128)(2,1)}) fusion(bf16[4,8,32,2,8,64]{5,4,2,3,1,0:T(8,128)(2,1)} %gather_fusion.2, pred[4]{0:T(512)(128)(4,1)S(1)} %get-tuple-element.17, bf16[4,8,32,2,8,64]{5,4,2,3,1,0:T(8,128)(2,1)} %gather_fusion.1, pred[4]{0:T(512)(128)(4,1)S(1)} %get-tuple-element.6), kind=kLoop, calls=%fused_computation.11 | loop fusion | flops 2097152 | bytes 8388616 | tf_op jit(solution)/shard_map/jit(_take)/select_n | solution.py:108
  179.3 6.8 %copy.101 = bf16[4,8,32,2,8,64]{5,1,0,4,2,3:T(8,128)(2,1)} copy(bf16[4,8,32,2,8,64]{5,4,2,3,1,0:T(8,128)(2,1)S(1)} %get-tuple-element.25) | data formatting | bytes 4194304 | tf_op jit(solution)/shard_map/jit(_take)/select_n | solution.py:108
  186.1 3.0 %fusion.54 = (f32[32,8,8]{2,1,0:T(8,128)S(1)}, f32[32,8,8,32]{3,2,1,0:T(8,128)S(1)}) fusion(bf16[32,32,2,8,64]{4,0,3,1,2:T(8,128)(2,1)} %bitcast.125, bf16[8,32,8,64]{3,2,1,0:T(8,128)(2,1)S(1)} %reshape_squeeze.7), kind=kOutput, calls=%fused_computation.88 | convolution fusion | flops 8585247 | bytes 2629632 | tf_op jit(solution)/shard_map/sub | solution.py:26
  189.1 2.3 %fusion.29 = bf16[8,32,8,64]{3,0,2,1:T(8,128)(2,1)S(1)} fusion(bf16[32,32,2,8,64]{4,0,3,1,2:T(8,128)(2,1)} %bitcast.126, f32[32,8,8,32]{3,2,1,0:T(8,128)S(1)} %get-tuple-element.20, f32[32,8,8]{2,1,0:T(8,128)S(1)} %get-tuple-element.19), kind=kOutput, calls=%fused_computation.50 | convolution fusion | flops 8650752 | bytes 2629632 | tf_op jit(solution)/shard_map/lhqk,klhd->qlhd/dot_general | solution.py:120
  191.8 9.2 %copy.102 = bf16[4,8,32,2,8,64]{5,1,0,4,2,3:T(8,128)(2,1)} copy(bf16[4,8,32,2,8,64]{5,4,2,3,1,0:T(8,128)(2,1)} %get-tuple-element.26) | data formatting | bytes 4194304 | tf_op jit(solution)/shard_map/jit(_take)/select_n | solution.py:108
  201.0 3.9 %fusion.55 = (f32[32,8,8]{2,1,0:T(8,128)S(1)}, f32[32,8,8,32]{3,2,1,0:T(8,128)}) fusion(bf16[32,32,2,8,64]{4,0,3,1,2:T(8,128)(2,1)} %bitcast.127, bf16[8,32,8,64]{3,2,1,0:T(8,128)(2,1)S(1)} %reshape_squeeze.6), kind=kOutput, calls=%fused_computation.89 | convolution fusion | flops 8585247 | bytes 2629632 | tf_op jit(solution)/shard_map/sub | solution.py:26
  204.9 2.7 %fusion.30 = bf16[8,32,8,64]{3,0,2,1:T(8,128)(2,1)S(1)} fusion(bf16[32,32,2,8,64]{4,0,3,1,2:T(8,128)(2,1)} %bitcast.128, f32[32,8,8,32]{3,2,1,0:T(8,128)} %get-tuple-element.22, f32[32,8,8]{2,1,0:T(8,128)S(1)} %get-tuple-element.21), kind=kOutput, calls=%fused_computation.51 | convolution fusion | flops 8650752 | bytes 3416064 | tf_op jit(solution)/shard_map/lhqk,klhd->qlhd/dot_general | solution.py:120
  208.5 2.2 %reshape.85 = bf16[8,32,512]{2,1,0:T(8,128)(2,1)} reshape(bf16[8,32,8,64]{3,2,1,0:T(8,128)(2,1)} %copy.70) | data formatting | bytes 524288 | tf_op jit(solution)/shard_map/reshape | solution.py:123
  (50 shorter events, 16.6 us)
Async XLA Ops:
  10.1 2.3 %copy-start.5 = (bf16[16,32,1024]{2,1,0:T(8,128)(2,1)S(1)}, bf16[16,32,1024]{2,1,0:T(8,128)(2,1)}, u32[]{:S(2)}) copy-start(bf16[16,32,1024]{2,1,0:T(8,128)(2,1)} %param.8) | copy-start | bytes 3145732
  10.1 2.3 %copy-start.7 = (f32[1024]{0:T(1024)S(1)}, f32[1024]{0:T(1024)}, u32[]{:S(2)}) copy-start(f32[1024]{0:T(1024)} %param.9) | copy-start | bytes 12292
  52.8 39.6 %all-to-all-start.1 = ((bf16[64,32,128]{2,1,0:T(8,128)(2,1)}), bf16[64,32,128]{2,1,0:T(8,128)(2,1)S(1)}, u32[]{:S(2)}, u32[]{:S(2)}) async-start(bf16[64,32,128]{2,1,0:T(8,128)(2,1)} %bitcast.9), calls=%async_computation.1 | async-start | bytes 1048576 | tf_op jit(solution)/shard_map/all_to_all | solution.py:76
  60.7 5.0 %copy-start.3 = (bf16[16,32,3,512]{3,1,2,0:T(8,128)(2,1)}, bf16[16,32,3,512]{3,1,2,0:T(8,128)(2,1)S(1)}, u32[]{:S(2)}) copy-start(bf16[16,32,3,512]{3,1,2,0:T(8,128)(2,1)S(1)} %fusion.18) | copy-start | bytes 4718596
  60.8 65.8 %collective-permute-start.2 = (bf16[16,32,2,512]{3,1,2,0:T(8,128)(2,1)S(1)}, bf16[16,32,2,512]{3,1,2,0:T(8,128)(2,1)}, u32[]{:S(2)}, u32[]{:S(2)}) collective-permute-start(bf16[16,32,2,512]{3,1,2,0:T(8,128)(2,1)S(1)} %slice.70), channel_id=1, source_target_pairs={{0,8},{8,0},{16,24},{24,16},{1,9},{9,1},{17,25},{25,17},{2,10},{10... | collective-permute-start | bytes 3145736 | tf_op jit(solution)/shard_map/ppermute | solution.py:21
  62.3 58.7 %collective-permute-start = (bf16[16,32,2,512]{3,1,2,0:T(8,128)(2,1)S(1)}, bf16[16,32,2,512]{3,1,2,0:T(8,128)(2,1)}, u32[]{:S(2)}, u32[]{:S(2)}) collective-permute-start(bf16[16,32,2,512]{3,1,2,0:T(8,128)(2,1)S(1)} %slice.70), channel_id=1, source_target_pairs={{0,4},{1,5},{2,6},{3,7},{4,0},{5,1},{6,2},{7,3},{8,12},{9,13},{10,... | collective-permute-start | bytes 3145736 | tf_op jit(solution)/shard_map/ppermute | solution.py:15
  97.5 3.3 %copy-start.4 = (bf16[8,256,2,64]{3,2,1,0:T(2,128)(2,1)S(1)}, bf16[8,256,2,64]{3,2,1,0:T(2,128)(2,1)}, u32[]{:S(2)}) copy-start(bf16[8,256,2,64]{3,2,1,0:T(2,128)(2,1)} %reshape.77) | copy-start | bytes 1572868
  102.4 27.5 %all-to-all-start.3 = ((bf16[8,256,128]{2,0,1:T(8,128)(2,1)}), bf16[8,256,128]{2,0,1:T(8,128)(2,1)S(1)}, u32[]{:S(2)}, u32[]{:S(2)}) async-start(bf16[8,256,128]{2,0,1:T(8,128)(2,1)} %copy.62), calls=%async_computation.3 | async-start | bytes 1048576 | tf_op jit(solution)/shard_map/all_to_all | solution.py:81
  121.0 9.8 %collective-permute-start.1 = (bf16[16,32,2,512]{3,1,2,0:T(8,128)(2,1)}, bf16[16,32,2,512]{3,1,2,0:T(8,128)(2,1)}, u32[]{:S(2)}, u32[]{:S(2)}) collective-permute-start(bf16[16,32,2,512]{3,1,2,0:T(8,128)(2,1)} %collective-permute-done), channel_id=1, source_target_pairs={{0,8},{8,0},{16,24},{24,16},{1,9},{9,1},{17,25},{25,17},{2,10},{10... | collective-permute-start | bytes 3145736 | tf_op jit(solution)/shard_map/ppermute | solution.py:21
  125.9 0.7 copy-start.6
  125.9 0.7 copy-start.8
  141.9 3.3 %copy-start = (bf16[32,32,2,512]{3,1,2,0:T(8,128)(2,1)S(1)}, bf16[32,32,2,512]{3,1,2,0:T(8,128)(2,1)}, u32[]{:S(2)}) copy-start(bf16[32,32,2,512]{3,1,2,0:T(8,128)(2,1)} %maximum_select_fusion.1) | copy-start | bytes 6291460
  204.9 5.8 %copy-start.1 = (bf16[1024,1024]{1,0:T(8,128)(2,1)S(1)}, bf16[1024,1024]{1,0:T(8,128)(2,1)}, u32[]{:S(2)}) copy-start(bf16[1024,1024]{1,0:T(8,128)(2,1)} %param.11) | copy-start | bytes 6291460
  208.5 3.9 %slice-start = ((bf16[1024,1024]{1,0:T(8,128)(2,1)}), bf16[512,1024]{1,0:T(8,128)(2,1)S(1)}, s32[]{:S(2)}) async-start(bf16[1024,1024]{1,0:T(8,128)(2,1)} %param.11), calls=%async_computation.4 | async-start | bytes 2097152 | tf_op jit(solution)/shard_map/slice | solution.py:125
  210.7 1.7 copy-start.2
where the time goes:
time: 215 us; the launch traced here: 214 us
  local copies, waits for them, and re-layouts  72.5 us (34%)
  waiting for transfers between devices  40.3 us (19%)
  blocking collectives  37.3 us (17%)
  other arithmetic  24.5 us (11%)
  matrix products  22.2 us (10%)
  starting transfers between devices  16.9 us (8%)
    all_to_all x1, waiting for transfers between devices, on_device(): lax.all_to_all(zonal_part[0], 'lon', split_axis=0, concat_axis=1, tiled=T...  26.7 us
    all_to_all x1, blocking collectives, on_device(): lax.all_to_all(zonal_part[1], 'lon', split_axis=0, concat_axis=1, tiled=T...  19.8 us
    all_to_all x1, blocking collectives, on_device(): lax.all_to_all(zonal_part[2], 'lon', split_axis=0, concat_axis=1, tiled=T...  17.5 us
    select_n x2, local copies, waits for them, and re-layouts, on_device(): jnp.take(column, picked, axis=0)  16 us
    ppermute x1, waiting for transfers between devices, shifted(): lax.ppermute(shard, axis, [(i, (i + by) % devices) for i in range(devices)])  13.7 us
    gather x2, local copies, waits for them, and re-layouts, on_device(): jnp.take(column, picked, axis=0)  12.8 us
    reshape x1, local copies, waits for them, and re-layouts, on_device(): column = column.reshape(block_total, BM, lon_count, 2, column_heads, HD)  11.2 us
    unnamed x19, local copies, waits for them, and re-layouts  8.72 us
  transfers between devices with their start and end apart: 5, of which 2 were waited for; matrix products, arithmetic and copies ran while one was open for 10% of the time, Pallas kernels for 0%

commit v1 on v0

--- a/solution.py
+++ b/solution.py
@@ -74,7 +74,12 @@
     ).astype(jnp.bfloat16)
     query_all, key_all, value_all = (
         lax.all_to_all(zonal_part[0], "lon", split_axis=0, concat_axis=1, tiled=True),
-        lax.all_to_all(zonal_part[1], "lon", split_axis=0, concat_axis=1, tiled=True),
+        jnp.concatenate(
+            lax.all_to_all(
+                jnp.stack(jnp.split(zonal_part[1], lax.axis_size("lon"), axis=0)), "lon", 0, 0
+            ),
+            axis=1,
+        ),
         lax.all_to_all(zonal_part[2], "lon", split_axis=0, concat_axis=1, tiled=True),
     )
     zonal_items = zonal_attend(query_all, key_all, value_all)

time: 215 us -> 224 us (1.042)
  blocking collectives: 37.3 us -> 18.3 us
  waiting for transfers between devices: 40.3 us -> 57.7 us
  local copies, waits for them, and re-layouts: 72.5 us -> 80 us
  starting transfers between devices: 16.9 us -> 20.8 us
    all_to_all x2 -> x1, blocking collectives: 37.3 us -> 18.3 us  [on_device(): lax.all_to_all(zonal_part[0], 'lon', split_axis=0, concat_axis=1, tiled=T...]
    all_to_all x1, waiting for transfers between devices: 0.01 us -> 9.05 us  [on_device(): lax.all_to_all(zonal_items, 'lon', split_axis=1, concat_axis=0, tiled=True)]
    all_to_all x1 -> x2, waiting for transfers between devices: 26.7 us -> 34.9 us  [the longest x1 22.3 us: on_device(): lax.all_to_all(zonal_part[2], 'lon', split_axis=0, concat_axis=1, tiled=T...]
    all_to_all x1 -> x2, starting transfers between devices: 4.07 us -> 10.5 us  [the longest x1 6.37 us: on_device(): lax.all_to_all(jnp.stack(jnp.split(zonal_part[1], lax.axis_size('lon'), a...]
    unnamed x19 -> x28, local copies, waits for them, and re-layouts: 8.72 us -> 14.2 us
    reshape x1, local copies, waits for them, and re-layouts: 2.44 us -> 0.04 us  [on_device(): jnp.concatenate(lax.all_to_all(jnp.stack(jnp.split(zonal_part[1], lax.axi...]
    select_n x1 -> x2, other arithmetic: 6.22 us -> 5.31 us  [on_device(): jnp.take(column, picked, axis=0)]
  transfers between devices with their start and end apart: 5 -> 6, of which waited for: 2 -> 4; matrix products, arithmetic and copies ran while one was open for 10% -> 11% of each run, Pallas kernels for 0% -> 0%
where the time goes in v1:
time: 224 us; the launch traced here: 222 us
  local copies, waits for them, and re-layouts  80 us (36%)
  waiting for transfers between devices  57.7 us (26%)
  other arithmetic  22.3 us (10%)
  matrix products  22.2 us (10%)
  starting transfers between devices  20.8 us (9%)
  blocking collectives  18.3 us (8%)
    all_to_all x1, waiting for transfers between devices, on_device(): lax.all_to_all(zonal_part[2], 'lon', split_axis=0, concat_axis=1, tiled=T...  22.3 us
    all_to_all x1, blocking collectives, on_device(): lax.all_to_all(zonal_part[0], 'lon', split_axis=0, concat_axis=1, tiled=T...  18.3 us
    unnamed x28, local copies, waits for them, and re-layouts  14.2 us
    select_n x2, local copies, waits for them, and re-layouts, on_device(): jnp.take(column, picked, axis=0)  13.9 us
    ppermute x1, waiting for transfers between devices, shifted(): lax.ppermute(shard, axis, [(i, (i + by) % devices) for i in range(devices)])  13.7 us
    gather x2, local copies, waits for them, and re-layouts, on_device(): jnp.take(column, picked, axis=0)  12.9 us
    all_to_all x1, waiting for transfers between devices, on_device(): lax.all_to_all(jnp.stack(jnp.split(zonal_part[1], lax.axis_size('lon'), a...  12.5 us
    reshape x1, local copies, waits for them, and re-layouts, on_device(): column = column.reshape(block_total, BM, lon_count, 2, column_heads, HD)  11.2 us
  transfers between devices with their start and end apart: 6, of which 4 were waited for; matrix products, arithmetic and copies ran while one was open for 11% of the time, Pallas kernels for 0%

profile of v1, /device:TPU:1, one launch (start us, length us, event | category | flops | bytes accessed | tf_op | source)
XLA Modules:
  0.0 221.7 jit_solution(15346100354830885021)
XLA Ops:
  0.0 8.6 %copy.68 = bf16[1024,3072]{0,1:T(8,128)(2,1)} copy(bf16[1024,3072]{1,0:T(8,128)(2,1)} %param.10) | data formatting | bytes 12582912 | tf_op args[2]
  8.6 2.3 %slice.78 = bf16[1024,3,512]{0,2,1:T(8,128)(2,1)S(1)} slice(bf16[1024,3,1024]{0,2,1:T(8,128)(2,1)} %bitcast.128), slice={[0:1024], [0:3], [0:512]} | slice | bytes 6291456 | tf_op jit(solution)/shard_map/slice | solution.py:64
  18.3 6.4 %all-to-all-start.2 = ((bf16[8,8,32,128]{3,2,1,0:T(8,128)(2,1)}), bf16[8,8,32,128]{3,2,1,0:T(8,128)(2,1)S(1)}, u32[]{:S(2)}, u32[]{:S(2)}) async-start(bf16[8,8,32,128]{3,2,1,0:T(8,128)(2,1)} %constant_dynamic-update-slice_fusion), calls=%async_computation.2 | async-start | bytes 1048576 | tf_op jit(solution)/shard_map/all_to_all | solution.py:78
  25.5 12.5 %all-to-all-done.2 = bf16[8,8,32,128]{3,2,1,0:T(8,128)(2,1)S(1)} async-done(((bf16[8,8,32,128]{3,2,1,0:T(8,128)(2,1)}), bf16[8,8,32,128]{3,2,1,0:T(8,128)(2,1)S(1)}, u32[]{:S(2)}, u32[]{:S(2)}) %all-to-all-start.2) | async-done | bytes 524320 | tf_op jit(solution)/shard_map/all_to_all | solution.py:78
  38.1 18.3 %all_to_all.50 = bf16[64,32,128]{2,1,0:T(8,128)(2,1)S(1)} all-to-all(bf16[64,32,128]{2,1,0:T(8,128)(2,1)S(1)} %bitcast.140), channel_id=1, replica_groups=mesh['lat'=4,'lon'=8] {'lon'}, dimensions={0} | all-to-all | bytes 1048576 | tf_op jit(solution)/shard_map/all_to_all | solution.py:76
  56.4 4.1 %all-to-all-start = ((bf16[64,32,128]{2,1,0:T(8,128)(2,1)}), bf16[64,32,128]{2,1,0:T(8,128)(2,1)}, u32[]{:S(2)}, u32[]{:S(2)}) async-start(bf16[64,32,128]{2,1,0:T(8,128)(2,1)} %bitcast.6), calls=%async_computation | async-start | bytes 1048576 | tf_op jit(solution)/shard_map/all_to_all | solution.py:83
  60.6 3.8 %fusion.18 = bf16[16,32,3,512]{3,1,2,0:T(8,128)(2,1)S(1)} fusion(bf16[1024,3,1024]{0,2,1:T(8,128)(2,1)} %bitcast.129, bf16[16,32,1024]{2,1,0:T(8,128)(2,1)S(1)} %copy-done.6, f32[1024]{0:T(1024)S(1)} %copy-done.8, f32[16,32]{1,0:T(8,128)S(1)} %add_rsqrt_fusion), kind=kOutput, calls=%fused_computation.38 | convolution fusion | flops 1613496320 | bytes 5773312 | tf_op jit(solution)/shard_map/rld,dtc->rltc/dot_general | solution.py:72
  65.5 2.3 %collective-permute-start = (bf16[16,32,2,512]{3,1,2,0:T(8,128)(2,1)S(1)}, bf16[16,32,2,512]{3,1,2,0:T(8,128)(2,1)}, u32[]{:S(2)}, u32[]{:S(2)}) collective-permute-start(bf16[16,32,2,512]{3,1,2,0:T(8,128)(2,1)S(1)} %slice.82), channel_id=1, source_target_pairs={{0,4},{1,5},{2,6},{3,7},{4,0},{5,1},{6,2},{7,3},{8,12},{9,13},{10,... | collective-permute-start | bytes 3145736 | tf_op jit(solution)/shard_map/ppermute | solution.py:15
  71.4 2.4 %reshape.93 = bf16[8,256,2,64]{3,2,1,0:T(2,128)(2,1)S(1)} reshape(bf16[8,8,32,128]{3,2,1,0:T(8,128)(2,1)} %copy.71) | data formatting | bytes 1048576 | tf_op jit(solution)/shard_map/reshape | solution.py:33
  73.8 22.3 %all-to-all-done = bf16[64,32,128]{2,1,0:T(8,128)(2,1)} async-done(((bf16[64,32,128]{2,1,0:T(8,128)(2,1)}), bf16[64,32,128]{2,1,0:T(8,128)(2,1)}, u32[]{:S(2)}, u32[]{:S(2)}) %all-to-all-start) | async-done | bytes 524320 | tf_op jit(solution)/shard_map/all_to_all | solution.py:83
  98.0 3.2 %reshape.92 = bf16[8,256,2,64]{3,2,1,0:T(2,128)(2,1)} reshape(bf16[8,8,32,128]{3,2,1,0:T(8,128)(2,1)} %copy.70) | data formatting | bytes 1048576 | tf_op jit(solution)/shard_map/reshape | solution.py:35
  101.9 3.2 %fusion.57 = (f32[8,2,256]{2,1,0:T(2,128)S(1)}, f32[8,2,256,256]{2,3,1,0:T(8,128)S(1)}) fusion(f32[8,2,256,256]{2,3,1,0:T(8,128)S(1)} %fusion.36), kind=kOutput, calls=%fused_computation.99 | output fusion | flops 4194559 | bytes 8404992 | tf_op jit(solution)/shard_map/sub | solution.py:26
  105.2 13.7 %collective-permute-done = bf16[16,32,2,512]{3,1,2,0:T(8,128)(2,1)} collective-permute-done((bf16[16,32,2,512]{3,1,2,0:T(8,128)(2,1)S(1)}, bf16[16,32,2,512]{3,1,2,0:T(8,128)(2,1)}, u32[]{:S(2)}, u32[]{:S(2)}) %collective-permute-start) | collective-permute-done | bytes 1048608 | tf_op jit(solution)/shard_map/ppermute | solution.py:15
  122.6 3.7 %all-to-all-start.3 = ((bf16[8,256,128]{2,0,1:T(8,128)(2,1)}), bf16[8,256,128]{2,0,1:T(8,128)(2,1)S(1)}, u32[]{:S(2)}, u32[]{:S(2)}) async-start(bf16[8,256,128]{2,0,1:T(8,128)(2,1)} %copy.77), calls=%async_computation.3 | async-start | bytes 1048576 | tf_op jit(solution)/shard_map/all_to_all | solution.py:86
  128.2 3.2 %maximum_select_fusion.1 = bf16[32,32,2,512]{3,1,2,0:T(8,128)(2,1)} fusion(bf16[16,32,2,512]{3,1,2,0:T(8,128)(2,1)} %collective-permute-done.2, bf16[16,32,2,512]{3,1,2,0:T(8,128)(2,1)S(1)} %slice.82, pred[]{:T(512)S(6)} %eq.8), kind=kLoop, calls=%fused_computation.31 | loop fusion | flops 3145728 | bytes 4194305 | tf_op jit(solution)/shard_map/jit(_where)/select_n | solution.py:93
  131.4 9.0 %all-to-all-done.3 = bf16[8,256,128]{2,0,1:T(8,128)(2,1)S(1)} async-done(((bf16[8,256,128]{2,0,1:T(8,128)(2,1)}), bf16[8,256,128]{2,0,1:T(8,128)(2,1)S(1)}, u32[]{:S(2)}, u32[]{:S(2)}) %all-to-all-start.3) | async-done | bytes 524320 | tf_op jit(solution)/shard_map/all_to_all | solution.py:86
  141.4 2.6 %maximum_select_fusion = bf16[32,32,2,512]{3,1,2,0:T(8,128)(2,1)S(1)} fusion(bf16[16,32,2,512]{3,1,2,0:T(8,128)(2,1)} %collective-permute-done.1, bf16[16,32,2,512]{3,1,2,0:T(8,128)(2,1)} %collective-permute-done, pred[]{:T(512)S(6)} %eq.8), kind=kLoop, calls=%fused_computation.30 | loop fusion | flops 3145728 | bytes 4194305 | tf_op jit(solution)/shard_map/jit(_where)/select_n | solution.py:93
  143.9 2.5 %copy.81 = bf16[32,32,2,512]{3,0,2,1:T(8,128)(2,1)} copy(bf16[32,32,2,512]{3,1,2,0:T(8,128)(2,1)S(1)} %maximum_select_fusion) | data formatting | bytes 4194304 | tf_op jit(solution)/shard_map/jit(_where)/select_n | solution.py:93
  148.7 3.7 %fusion.15 = bf16[32,32,2,512]{3,1,2,0:T(8,128)(2,1)} fusion(bf16[32,32,2,512]{3,1,2,0:T(8,128)(2,1)S(1)} %gather_fusion, pred[32]{0:T(512)(128)(4,1)S(1)} %get-tuple-element.10), kind=kLoop, calls=%fused_computation.35 | loop fusion | flops 1048576 | bytes 4194336 | tf_op jit(solution)/shard_map/jit(_take)/select_n | solution.py:103
  152.4 3.3 %rev.3 = bf16[32,32,2,512]{3,1,2,0:T(8,128)(2,1)} reverse(bf16[32,32,2,512]{3,1,2,0:T(8,128)(2,1)} %fusion.15), dimensions={0} | reverse | bytes 4194304 | tf_op jit(solution)/shard_map/rev | solution.py:103
  155.8 3.9 %pad_maximum_fusion = bf16[64,32,2,512]{3,1,2,0:T(8,128)(2,1)} fusion(bf16[32,32,2,512]{3,1,2,0:T(8,128)(2,1)S(1)} %copy-done, bf16[32,32,2,512]{3,1,2,0:T(8,128)(2,1)} %rev.3), kind=kLoop, calls=%fused_computation.6 | loop fusion | flops 2097152 | bytes 8388608 | tf_op jit(solution)/shard_map/concatenate | solution.py:104
  159.7 11.2 %reshape.98 = bf16[8,8,32,2,8,64]{5,4,2,3,1,0:T(8,128)(2,1)} reshape(bf16[64,32,2,512]{3,1,2,0:T(8,128)(2,1)} %pad_maximum_fusion) | data formatting | bytes 8388608 | tf_op jit(solution)/shard_map/reshape | solution.py:106
  170.9 6.4 %gather_fusion.1 = bf16[4,8,32,2,8,64]{5,4,2,3,1,0:T(8,128)(2,1)} fusion(bf16[8,8,32,2,8,64]{5,4,2,3,1,0:T(8,128)(2,1)} %reshape.98, s32[1024]{0:T(1024)S(1)} %get-tuple-element.33), kind=kCustom, calls=%fused_computation.clone | custom fusion | bytes 4194320 | tf_op jit(solution)/shard_map/jit(_take)/gather | solution.py:113
  177.3 2.7 %broadcast_select_fusion.1 = bf16[4,8,32,2,8,64]{5,4,2,3,1,0:T(8,128)(2,1)S(1)} fusion(bf16[4,8,32,2,8,64]{5,4,2,3,1,0:T(8,128)(2,1)} %gather_fusion.1, pred[4]{0:T(512)(128)(4,1)S(1)} %get-tuple-element.6), kind=kLoop, calls=%fused_computation.12 | loop fusion | flops 1048576 | bytes 4194308 | tf_op jit(solution)/shard_map/jit(_take)/select_n | solution.py:113
  180.0 6.8 %copy.117 = bf16[4,8,32,2,8,64]{5,1,0,4,2,3:T(8,128)(2,1)} copy(bf16[4,8,32,2,8,64]{5,4,2,3,1,0:T(8,128)(2,1)S(1)} %broadcast_select_fusion.1) | data formatting | bytes 4194304 | tf_op jit(solution)/shard_map/jit(_take)/select_n | solution.py:113
  186.8 3.0 %fusion.56 = (f32[32,8,8]{2,1,0:T(8,128)S(1)}, f32[32,8,8,32]{3,2,1,0:T(8,128)S(1)}) fusion(bf16[32,32,2,8,64]{4,0,3,1,2:T(8,128)(2,1)} %bitcast.130, bf16[8,32,8,64]{3,2,1,0:T(8,128)(2,1)S(1)} %reshape_squeeze.6), kind=kOutput, calls=%fused_computation.98 | convolution fusion | flops 8585247 | bytes 2629632 | tf_op jit(solution)/shard_map/sub | solution.py:26
  189.8 2.3 %fusion.30 = bf16[8,32,8,64]{3,0,2,1:T(8,128)(2,1)S(1)} fusion(bf16[32,32,2,8,64]{4,0,3,1,2:T(8,128)(2,1)} %bitcast.131, f32[32,8,8,32]{3,2,1,0:T(8,128)S(1)} %get-tuple-element.29, f32[32,8,8]{2,1,0:T(8,128)S(1)} %get-tuple-element.28), kind=kOutput, calls=%fused_computation.51 | convolution fusion | flops 8650752 | bytes 2629632 | tf_op jit(solution)/shard_map/lhqk,klhd->qlhd/dot_general | solution.py:125
  192.5 6.4 %gather_fusion.2 = bf16[4,8,32,2,8,64]{5,4,2,3,1,0:T(8,128)(2,1)} fusion(bf16[8,8,32,2,8,64]{5,4,2,3,1,0:T(8,128)(2,1)} %reshape.98, s32[1024]{0:T(1024)S(1)} %get-tuple-element.32), kind=kCustom, calls=%fused_computation.1.clone | custom fusion | bytes 4194320 | tf_op jit(solution)/shard_map/jit(_take)/gather | solution.py:113
  198.9 2.7 %broadcast_select_fusion = bf16[4,8,32,2,8,64]{5,4,2,3,1,0:T(8,128)(2,1)S(1)} fusion(bf16[4,8,32,2,8,64]{5,4,2,3,1,0:T(8,128)(2,1)} %gather_fusion.2, pred[4]{0:T(512)(128)(4,1)S(1)} %get-tuple-element.24), kind=kLoop, calls=%fused_computation.11 | loop fusion | flops 1048576 | bytes 4194308 | tf_op jit(solution)/shard_map/jit(_take)/select_n | solution.py:113
  201.6 7.1 %copy.116 = bf16[4,8,32,2,8,64]{5,1,0,4,2,3:T(8,128)(2,1)} copy(bf16[4,8,32,2,8,64]{5,4,2,3,1,0:T(8,128)(2,1)S(1)} %broadcast_select_fusion) | data formatting | bytes 4194304 | tf_op jit(solution)/shard_map/jit(_take)/select_n | solution.py:113
  208.6 3.9 %fusion.55 = (f32[32,8,8]{2,1,0:T(8,128)S(1)}, f32[32,8,8,32]{3,2,1,0:T(8,128)}) fusion(bf16[32,32,2,8,64]{4,0,3,1,2:T(8,128)(2,1)} %bitcast.132, bf16[8,32,8,64]{3,2,1,0:T(8,128)(2,1)S(1)} %reshape_squeeze.7), kind=kOutput, calls=%fused_computation.97 | convolution fusion | flops 8585247 | bytes 2629632 | tf_op jit(solution)/shard_map/sub | solution.py:26
  212.5 2.7 %fusion.29 = bf16[8,32,8,64]{3,0,2,1:T(8,128)(2,1)S(1)} fusion(bf16[32,32,2,8,64]{4,0,3,1,2:T(8,128)(2,1)} %bitcast.133, f32[32,8,8,32]{3,2,1,0:T(8,128)} %get-tuple-element.27, f32[32,8,8]{2,1,0:T(8,128)S(1)} %get-tuple-element.26), kind=kOutput, calls=%fused_computation.50 | convolution fusion | flops 8650752 | bytes 3416064 | tf_op jit(solution)/shard_map/lhqk,klhd->qlhd/dot_general | solution.py:125
  (62 shorter events, 31.0 us)
Async XLA Ops:
  8.6 2.3 %copy-start.5 = (bf16[16,32,1024]{2,1,0:T(8,128)(2,1)S(1)}, bf16[16,32,1024]{2,1,0:T(8,128)(2,1)}, u32[]{:S(2)}) copy-start(bf16[16,32,1024]{2,1,0:T(8,128)(2,1)} %param.8) | copy-start | bytes 3145732
  8.6 2.6 %copy-start.8 = (f32[1024]{0:T(1024)S(1)}, f32[1024]{0:T(1024)}, u32[]{:S(2)}) copy-start(f32[1024]{0:T(1024)} %param.9) | copy-start | bytes 12292
  18.3 19.8 %all-to-all-start.2 = ((bf16[8,8,32,128]{3,2,1,0:T(8,128)(2,1)}), bf16[8,8,32,128]{3,2,1,0:T(8,128)(2,1)S(1)}, u32[]{:S(2)}, u32[]{:S(2)}) async-start(bf16[8,8,32,128]{3,2,1,0:T(8,128)(2,1)} %constant_dynamic-update-slice_fusion), calls=%async_computation.2 | async-start | bytes 1048576 | tf_op jit(solution)/shard_map/all_to_all | solution.py:78
  25.5 35.0 %copy-start.6 = (bf16[16,32,1024]{2,1,0:T(8,128)(2,1)S(1)}, bf16[16,32,1024]{2,1,0:T(8,128)(2,1)}, u32[]{:S(2)}) copy-start(bf16[16,32,1024]{2,1,0:T(8,128)(2,1)} %param.8) | copy-start | bytes 3145732
  56.4 39.8 %all-to-all-start = ((bf16[64,32,128]{2,1,0:T(8,128)(2,1)}), bf16[64,32,128]{2,1,0:T(8,128)(2,1)}, u32[]{:S(2)}, u32[]{:S(2)}) async-start(bf16[64,32,128]{2,1,0:T(8,128)(2,1)} %bitcast.6), calls=%async_computation | async-start | bytes 1048576 | tf_op jit(solution)/shard_map/all_to_all | solution.py:83
  64.4 1.1 copy-start.3
  65.5 53.4 %collective-permute-start = (bf16[16,32,2,512]{3,1,2,0:T(8,128)(2,1)S(1)}, bf16[16,32,2,512]{3,1,2,0:T(8,128)(2,1)}, u32[]{:S(2)}, u32[]{:S(2)}) collective-permute-start(bf16[16,32,2,512]{3,1,2,0:T(8,128)(2,1)S(1)} %slice.82), channel_id=1, source_target_pairs={{0,4},{1,5},{2,6},{3,7},{4,0},{5,1},{6,2},{7,3},{8,12},{9,13},{10,... | collective-permute-start | bytes 3145736 | tf_op jit(solution)/shard_map/ppermute | solution.py:15
  67.8 60.4 %collective-permute-start.2 = (bf16[16,32,2,512]{3,1,2,0:T(8,128)(2,1)S(1)}, bf16[16,32,2,512]{3,1,2,0:T(8,128)(2,1)}, u32[]{:S(2)}, u32[]{:S(2)}) collective-permute-start(bf16[16,32,2,512]{3,1,2,0:T(8,128)(2,1)S(1)} %slice.82), channel_id=1, source_target_pairs={{0,8},{8,0},{16,24},{24,16},{1,9},{9,1},{17,25},{25,17},{2,10},{10... | collective-permute-start | bytes 3145736 | tf_op jit(solution)/shard_map/ppermute | solution.py:21
  101.9 19.1 %copy-start.4 = (bf16[8,256,2,64]{3,2,1,0:T(2,128)(2,1)S(1)}, bf16[8,256,2,64]{3,2,1,0:T(2,128)(2,1)}, u32[]{:S(2)}) copy-start(bf16[8,256,2,64]{3,2,1,0:T(2,128)(2,1)} %reshape.92) | copy-start | bytes 1572868
  118.9 22.4 %collective-permute-start.1 = (bf16[16,32,2,512]{3,1,2,0:T(8,128)(2,1)}, bf16[16,32,2,512]{3,1,2,0:T(8,128)(2,1)}, u32[]{:S(2)}, u32[]{:S(2)}) collective-permute-start(bf16[16,32,2,512]{3,1,2,0:T(8,128)(2,1)} %collective-permute-done), channel_id=1, source_target_pairs={{0,8},{8,0},{16,24},{24,16},{1,9},{9,1},{17,25},{25,17},{2,10},{10... | collective-permute-start | bytes 3145736 | tf_op jit(solution)/shard_map/ppermute | solution.py:21
  122.6 17.8 %all-to-all-start.3 = ((bf16[8,256,128]{2,0,1:T(8,128)(2,1)}), bf16[8,256,128]{2,0,1:T(8,128)(2,1)S(1)}, u32[]{:S(2)}, u32[]{:S(2)}) async-start(bf16[8,256,128]{2,0,1:T(8,128)(2,1)} %copy.77), calls=%async_computation.3 | async-start | bytes 1048576 | tf_op jit(solution)/shard_map/all_to_all | solution.py:86
  127.4 0.7 copy-start.7
  127.4 0.7 copy-start.9
  152.4 3.3 %copy-start = (bf16[32,32,2,512]{3,1,2,0:T(8,128)(2,1)S(1)}, bf16[32,32,2,512]{3,1,2,0:T(8,128)(2,1)}, u32[]{:S(2)}) copy-start(bf16[32,32,2,512]{3,1,2,0:T(8,128)(2,1)} %maximum_select_fusion.1) | copy-start | bytes 6291460
  212.5 5.8 %copy-start.1 = (bf16[1024,1024]{1,0:T(8,128)(2,1)S(1)}, bf16[1024,1024]{1,0:T(8,128)(2,1)}, u32[]{:S(2)}) copy-start(bf16[1024,1024]{1,0:T(8,128)(2,1)} %param.11) | copy-start | bytes 6291460
  216.1 3.9 %slice-start = ((bf16[1024,1024]{1,0:T(8,128)(2,1)}), bf16[512,1024]{1,0:T(8,128)(2,1)S(1)}, s32[]{:S(2)}) async-start(bf16[1024,1024]{1,0:T(8,128)(2,1)} %param.11), calls=%async_computation.4 | async-start | bytes 2097152 | tf_op jit(solution)/shard_map/slice | solution.py:130
  218.3 1.7 copy-start.2
